TPU v7x, 128 devices: a whole 4x4x4 slice. The times are simulated.
128 devices in a mesh: req: 16 (over z, y), tp: 8 (over x, core).
Axes of the slice: x: 4, y: 4, z: 4, core: 2. Of those that a mesh axis runs over, the one named last changes fastest.
Arguments:
- hidden_in: bfloat16 [4096, 1024], P('req'), may hold values from -42 to 42
- prompt_kv: bfloat16 [2, 128, 512, 1024], P(None, 'req', None, 'tp'), may hold values from -9 to 9
- tail_kv: bfloat16 [2, 4096, 64, 1024], P(None, 'req', None, 'tp'), may hold values from -9 to 9
- group_of: int32 [4096], P('req'), may hold values from 0 to 7
- prompt_len: int32 [128], P('req'), may hold values from 64 to 512, as said below
- tail_len: int32 [4096], P('req'), may hold values from 0 to 63, as said below
- bucket_of: int32 [577], replicated, may hold values from 0 to 31, never falling along the last dimension, each value on 1 to 38 neighbouring positions
- bias_table: float32 [32, 16], P(None, 'tp'), may hold values from -6 to 302
- attn_gain: float32 [1024], replicated, may hold values from 0.1 to 1.9
- w_query: bfloat16 [1024, 1024], P(None, 'tp'), may hold values from -0.1875 to 0.1875
- w_key: bfloat16 [1024, 1024], P(None, 'tp'), may hold values from -0.1875 to 0.1875
- w_value: bfloat16 [1024, 1024], P(None, 'tp'), may hold values from -0.1875 to 0.1875
- w_out: bfloat16 [1024, 1024], P('tp'), may hold values from -0.75 to 0.75
- ffn_gain: float32 [1024], replicated, may hold values from 0.1 to 1.9
- router_weight: bfloat16 [1024, 16], replicated, may hold values from -0.1875 to 0.1875
- expert_ids: int32 [4096, 2], P('req'), may hold values from 0 to 15, all different within a row; in each aligned block of 256 rows (0 to 255, 256 to 511, ...) at most 40 rows name the same one
- w_gate: bfloat16 [16, 1024, 2816], P('req', None, 'tp'), may hold values from -0.1875 to 0.1875
- w_up: bfloat16 [16, 1024, 2816], P('req', None, 'tp'), may hold values from -0.1875 to 0.1875
- w_down: bfloat16 [16, 2816, 1024], P('req', 'tp'), may hold values from -0.109375 to 0.109375
- new_slot: int32 [4096], replicated, may hold values from 0 to 4095, as said below
Outputs:
- out_hidden: bfloat16 [4096, 1024], P('req')
- new_tail_kv: bfloat16 [2, 4096, 64, 1024], P(None, 'req', None, 'tp')
Inputs may be any that keep to these rules, and one draw needn't show every extreme that they name: `expert_ids`: in each replica's aligned block of 256 tokens no expert is named by more than 40 of them, a bound that some block reaches. `new_slot`: A permutation. Exactly 4 requests of each replica are movers; all movers of one replica go to one replica (possibly itself), each taking a slot that a mover of that replica leaves; every other request keeps its slot. `prompt_len`: each replica has a group of 512 rows. `tail_len`: each replica has a request of 63 own rows and one of none.
All inputs are finite; a program needn't handle non-finite values.
Results may differ from a plain program's by a relative error of at most 0.013.
Values may be sent and summed in bfloat16 or wider, within the bound.
A program may use at most 128 MiB of HBM per device.

v0:
```python
import jax
import jax.numpy as jnp
from jax import lax
from jax.sharding import PartitionSpec as P

HD = 64
TOP = 2
MIG = 4
EPS = 1e-06


def rms_scale(values, gain):
    v = values.astype(jnp.float32)
    return (v * lax.rsqrt(jnp.mean(v * v, axis=-1, keepdims=True) + EPS) * gain).astype(
        jnp.bfloat16
    )


def bias_lookup(distance, starts, finish, bias_table):
    within = (distance[..., None] >= starts) & (distance[..., None] < finish)
    return jnp.einsum(
        "rjk,kh->hrj", within.astype(jnp.float32), bias_table, precision=lax.Precision.HIGHEST
    )


def attention(
    hidden_in,
    prompt_kv,
    tail_kv,
    group_of,
    prompt_len,
    tail_len,
    bucket_of,
    bias_table,
    attn_gain,
    w_query,
    w_key,
    w_value,
):
    normed = rms_scale(hidden_in, attn_gain)
    query = jnp.dot(normed, w_query, preferred_element_type=jnp.float32).astype(jnp.bfloat16)
    key_new = jnp.dot(normed, w_key, preferred_element_type=jnp.float32).astype(jnp.bfloat16)
    value_new = jnp.dot(normed, w_value, preferred_element_type=jnp.float32).astype(jnp.bfloat16)
    rows = hidden_in.shape[0]
    heads_here = w_query.shape[1] // HD
    groups_here = prompt_kv.shape[1]
    prompt_rows = prompt_kv.shape[2]
    tail_rows = tail_kv.shape[2]
    span = bucket_of.shape[0]
    buckets = bias_table.shape[0]
    bucket_ids = jnp.arange(buckets, dtype=jnp.int32)
    starts = jnp.sum((bucket_of[:, None] < bucket_ids[None, :]).astype(jnp.int32), axis=0)
    finish = jnp.concatenate([starts[1:], jnp.full((1,), span, jnp.int32)])
    first_bias = jnp.sum(jnp.where((bucket_ids == bucket_of[0])[:, None], bias_table, 0.0), axis=0)
    scale = HD ** (-0.5)
    q = query.reshape(rows, heads_here, HD)
    pk = prompt_kv[0].reshape(groups_here, prompt_rows, heads_here, HD)
    pv = prompt_kv[1].reshape(groups_here, prompt_rows, heads_here, HD)
    tk = tail_kv[0].reshape(rows, tail_rows, heads_here, HD)
    tv = tail_kv[1].reshape(rows, tail_rows, heads_here, HD)
    kn = key_new.reshape(rows, heads_here, HD)
    vn = value_new.reshape(rows, heads_here, HD)
    group_hit = group_of[:, None] == jnp.arange(groups_here, dtype=jnp.int32)[None, :]
    own_len = jnp.sum(jnp.where(group_hit, prompt_len[None, :], 0), axis=1)
    pos = own_len + tail_len
    jpos = jnp.arange(prompt_rows, dtype=jnp.int32)
    pidx = jnp.clip(pos[:, None] - jpos[None, :], 0, span - 1)
    pbias = bias_lookup(pidx, starts, finish, bias_table)
    pmask = group_hit[:, :, None] & (jpos[None, None, :] < own_len[:, None, None])
    ps = (
        jnp.einsum("rhd,gjhd->hrgj", q, pk, preferred_element_type=jnp.float32) * scale
        + pbias[:, :, None, :]
    )
    ps = jnp.where(pmask[None], ps, -jnp.inf)
    tpos = jnp.arange(tail_rows, dtype=jnp.int32)
    tidx = jnp.clip(tail_len[:, None] - tpos[None, :], 0, span - 1)
    tbias = bias_lookup(tidx, starts, finish, bias_table)
    tmask = tpos[None, :] < tail_len[:, None]
    ts = jnp.einsum("rhd,rthd->hrt", q, tk, preferred_element_type=jnp.float32) * scale + tbias
    ts = jnp.where(tmask[None], ts, -jnp.inf)
    ns = (
        jnp.einsum("rhd,rhd->hr", q, kn, preferred_element_type=jnp.float32) * scale
        + first_bias[:, None]
    )
    top = jnp.maximum(jnp.maximum(jnp.max(ps, axis=(2, 3)), jnp.max(ts, axis=2)), ns)
    pe = jnp.exp(ps - top[:, :, None, None])
    te = jnp.exp(ts - top[:, :, None])
    ne = jnp.exp(ns - top)
    total = jnp.sum(pe, axis=(2, 3)) + jnp.sum(te, axis=2) + ne
    pw = (pe / total[:, :, None, None]).astype(jnp.bfloat16)
    tw = (te / total[:, :, None]).astype(jnp.bfloat16)
    nw = (ne / total).astype(jnp.bfloat16)
    head = jnp.einsum("hrgj,gjhd->rhd", pw, pv, preferred_element_type=jnp.float32)
    head = head + jnp.einsum("hrt,rthd->rhd", tw, tv, preferred_element_type=jnp.float32)
    head = head + jnp.einsum("hr,rhd->rhd", nw, vn, preferred_element_type=jnp.float32)
    head_out = head.reshape(rows, heads_here * HD).astype(jnp.bfloat16)
    return (head_out, key_new, value_new, tmask)


def body(
    hidden_in,
    prompt_kv,
    tail_kv,
    group_of,
    prompt_len,
    tail_len,
    bucket_of,
    bias_table,
    attn_gain,
    w_query,
    w_key,
    w_value,
    w_out,
    ffn_gain,
    router_weight,
    expert_ids,
    w_gate,
    w_up,
    w_down,
    new_slot,
):
    head_out, key_new, value_new, tmask = attention(
        hidden_in,
        prompt_kv,
        tail_kv,
        group_of,
        prompt_len,
        tail_len,
        bucket_of,
        bias_table,
        attn_gain,
        w_query,
        w_key,
        w_value,
    )
    rows = hidden_in.shape[0]
    width = hidden_in.shape[1]
    local_idx = jnp.arange(rows, dtype=jnp.int32)
    tail_rows = tail_kv.shape[2]
    write_row = jnp.arange(tail_rows, dtype=jnp.int32)[None, :] == tail_len[:, None]
    fresh = jnp.stack([key_new, value_new])[:, :, None, :]
    tail_new = jnp.where(write_row[None, :, :, None], fresh, tail_kv)
    partial_attn = jnp.dot(head_out, w_out, preferred_element_type=jnp.float32)
    attn = lax.psum(partial_attn, "tp")
    resid = (hidden_in.astype(jnp.float32) + attn).astype(jnp.bfloat16)
    normed2 = rms_scale(resid, ffn_gain)
    logits = jnp.dot(normed2, router_weight, preferred_element_type=jnp.float32)
    experts = router_weight.shape[1]
    expert_range = jnp.arange(experts, dtype=jnp.int32)
    first_hit = expert_ids[:, 0:1] == expert_range[None, :]
    second_hit = expert_ids[:, 1:2] == expert_range[None, :]
    picked_first = jnp.sum(jnp.where(first_hit, logits, 0.0), axis=1)
    picked_second = jnp.sum(jnp.where(second_hit, logits, 0.0), axis=1)
    gate_first = jax.nn.sigmoid(picked_first - picked_second)
    capacity = 5 * rows * TOP // (4 * experts)
    flat_e = expert_ids.reshape(-1)
    onehot = (flat_e[:, None] == expert_range[None, :]).astype(jnp.int32)
    slot_pos = jnp.sum((jnp.cumsum(onehot, axis=0) - 1) * onehot, axis=1)
    target = flat_e * capacity + slot_pos
    placed = (target[:, None] == jnp.arange(experts * capacity, dtype=jnp.int32)[None, :]).astype(
        jnp.bfloat16
    )
    doubled = jnp.repeat(normed2, TOP, axis=0)
    outgoing = (
        jnp.dot(placed.T, doubled, preferred_element_type=jnp.float32)
        .astype(jnp.bfloat16)
        .reshape(experts, capacity, width)
    )
    gate_mat = w_gate[0]
    up_mat = w_up[0]
    down_mat = w_down[0]
    received = lax.all_to_all(outgoing, "req", split_axis=0, concat_axis=0, tiled=True)
    flat = received.reshape(-1, received.shape[-1])
    gate_h = jnp.dot(flat, gate_mat, preferred_element_type=jnp.float32)
    up_h = jnp.dot(flat, up_mat, preferred_element_type=jnp.float32)
    act = (jax.nn.gelu(gate_h, approximate=True) * up_h).astype(jnp.bfloat16)
    summed = lax.psum(
        jnp.dot(act, down_mat, preferred_element_type=jnp.float32).astype(jnp.bfloat16), "tp"
    )
    back = summed.reshape(received.shape)
    result = lax.all_to_all(back, "req", split_axis=0, concat_axis=0, tiled=True)
    pair_out = jnp.dot(
        placed, result.reshape(experts * capacity, width), preferred_element_type=jnp.float32
    ).reshape(rows, TOP, width)
    mixed = (
        resid.astype(jnp.float32)
        + gate_first[:, None] * pair_out[:, 0]
        + (1.0 - gate_first)[:, None] * pair_out[:, 1]
    ).astype(jnp.bfloat16)
    replicas = lax.axis_size("req")
    me = lax.axis_index("req")
    total_reqs = new_slot.shape[0]
    everyone = jnp.arange(total_reqs, dtype=jnp.int32)
    leaving_all = new_slot // rows != everyone // rows
    rank_all = (
        jnp.cumsum(leaving_all.reshape(replicas, rows).astype(jnp.int32), axis=1) - 1
    ).reshape(-1)
    source_of = jnp.zeros((total_reqs,), jnp.int32).at[new_slot].set(everyone)
    first_slot = me * rows
    leaving = lax.dynamic_slice_in_dim(leaving_all, first_slot, rows, 0)
    my_rank = lax.dynamic_slice_in_dim(rank_all, first_slot, rows, 0)
    send_idx = (
        jnp.zeros((MIG,), jnp.int32)
        .at[jnp.where(leaving, my_rank, MIG)]
        .set(local_idx, mode="drop")
    )
    send_rows = mixed[send_idx]
    send_tail = jnp.swapaxes(tail_new[:, send_idx], 0, 1)
    got_rows, got_tail = (
        lax.all_gather(send_rows, "req", axis=0, tiled=True),
        lax.all_gather(send_tail, "req", axis=0, tiled=True),
    )
    count = jnp.sum(leaving.astype(jnp.int32))
    vacated = jnp.where(jnp.arange(MIG, dtype=jnp.int32) < count, send_idx, rows)
    source = source_of[first_slot + jnp.minimum(vacated, rows - 1)]
    position = source // rows * MIG + rank_all[source]
    position = jnp.clip(position, 0, got_rows.shape[0] - 1)
    out_hidden = mixed.at[vacated].set(got_rows[position], mode="drop")
    new_tail_kv = tail_new.at[:, vacated].set(jnp.swapaxes(got_tail[position], 0, 1), mode="drop")
    return (out_hidden, new_tail_kv)


def solution(mesh):
    return jax.shard_map(
        body,
        mesh=mesh,
        in_specs=(
            P("req", None),
            P(None, "req", None, "tp"),
            P(None, "req", None, "tp"),
            P("req"),
            P("req"),
            P("req"),
            P(),
            P(None, "tp"),
            P(),
            P(None, "tp"),
            P(None, "tp"),
            P(None, "tp"),
            P("tp", None),
            P(),
            P(),
            P("req", None),
            P("req", None, "tp"),
            P("req", None, "tp"),
            P("req", "tp", None),
            P(),
        ),
        out_specs=(P("req", None), P(None, "req", None, "tp")),
        check_vma=False,
    )
```

profile of v0, /device:TPU:6, one launch (start us, length us, event | category | flops | bytes accessed | tf_op | source)
XLA Modules:
  0.0 309.5 jit_solution(10653071250375701447)
XLA Ops:
  15.9 6.9 %fusion.8 = f32[2,256,512]{2,0,1:T(2,128)S(1)} fusion(s32[256,512]{1,0:T(8,128)S(1)} %subtract_clamp_fusion, s32[32]{0:T(128)S(1)} %pad_add_fusion, s32[32]{0:T(128)S(1)} %convert_reduce_fusion, f32[32,2]{0,1:T(2,128)} %param.27), kind=kOutput, calls=%fused_computation.35 | convolution fusion | flops 113246208 | bytes 1573376 | tf_op jit(solution)/shard_map/rjk,kh->hrj/dot_general | solution.py:21
  25.8 6.5 %fusion.89 = (bf16[1,256,64,128]{3,2,1,0:T(8,128)(2,1)}, bf16[1,256,64,128]{3,2,1,0:T(8,128)(2,1)}) fusion(bf16[2,256,64,128]{3,2,1,0:T(8,128)(2,1)} %param.22), kind=kLoop, calls=%fused_computation.187 | loop fusion | bytes 16777216 | tf_op jit(solution)/shard_map/slice | solution.py:59
  32.3 7.0 %copy.114 = bf16[1,256,64,128]{1,3,2,0:T(8,128)(2,1)} copy(bf16[1,256,64,128]{3,2,1,0:T(8,128)(2,1)} %get-tuple-element.12) | data formatting | bytes 8388608
  42.9 3.7 %multiply_reduce_fusion.1 = f32[2,256,64]{1,0,2:T(2,128)S(1)} fusion(bf16[2,256,64,64]{1,2,0,3:T(8,128)(2,1)} %bitcast.145, f32[2,256,64]{1,2,0:T(8,128)S(1)} %get-tuple-element.27), kind=kLoop, calls=%fused_computation.13 | loop fusion | flops 6258688 | bytes 4456448 | tf_op jit(solution)/shard_map/rhd,rthd->hrt/dot_general | solution.py:79
  47.6 2.2 fusion.5
  49.9 2.7 fusion.4
  54.7 6.9 %copy.116 = bf16[1,256,64,128]{1,3,2,0:T(8,128)(2,1)} copy(bf16[1,256,64,128]{3,2,1,0:T(8,128)(2,1)} %get-tuple-element.13) | data formatting | bytes 8388608
  63.6 2.3 copy.115
  65.9 3.2 %multiply_reduce_fusion = f32[256,2,64]{0,2,1:T(8,128)S(1)} fusion(bf16[256,2,64,64]{0,3,1,2:T(8,128)(2,1)} %bitcast.146, f32[256,2,64]{0,1,2:T(2,128)S(1)} %bitcast_convert_fusion), kind=kLoop, calls=%fused_computation.12 | loop fusion | flops 6258688 | bytes 4456448 | tf_op jit(solution)/shard_map/hrt,rthd->rhd/dot_general | solution.py:94
  69.2 5.1 %fusion.19 = bf16[256,2,64]{0,2,1:T(8,128)(2,1)S(1)} fusion(f32[256,2,64]{0,2,1:T(8,128)S(1)} %multiply_reduce_fusion, f32[2,256,8,512]{3,1,2,0:T(8,128)} %copy-done.1, f32[2,256]{1,0:T(2,128)S(1)} %copy-done.18, f32[2,256]{1,0:T(2,128)S(1)} %copy-done.13, f32[2,256,512]{2,1,0:T(8,128)S(1)} %copy.78, pred[256,8,512]{2,0,1:T(8,128)(4,1)S(1)} %broadcast_and_fusion, ...), kind=kOutput, calls=%fused_computation.52 | convolution fusion | flops 281182208 | bytes 11802624 | tf_op jit(solution)/shard_map/hrgj,gjhd->rhd/dot_general | solution.py:93
  77.6 60.5 %all-reduce.3.cloned.1.call-done = f32[256,1024]{1,0:T(8,128)} async-done(((f32[256,1024]{1,0:T(8,128)}), f32[256,1024]{1,0:T(8,128)}) %all-reduce.3.cloned.1.call-update) | async-done | bytes 1048592 | tf_op jit(solution)/shard_map/psum | solution.py:144
  141.6 3.2 %convolution_convert_fusion.1 = bf16[640,1024]{1,0:T(8,128)(2,1)} fusion(bf16[512,1024]{1,0:T(8,128)(2,1)} %reshape.353, s32[512]{0:T(512)S(1)} %multiply_add_fusion), kind=kOutput, calls=%fused_computation.28 | convolution fusion | flops 672071680 | bytes 2361344 | tf_op jit(solution)/shard_map/dot_general | solution.py:165
  144.9 7.0 %all-to-all-start = ((bf16[16,40,1024]{2,1,0:T(8,128)(2,1)}), bf16[16,40,1024]{2,1,0:T(8,128)(2,1)S(1)}, u32[]{:S(2)}, u32[]{:S(2)}) async-start(bf16[16,40,1024]{2,1,0:T(8,128)(2,1)} %bitcast.149), calls=%async_computation | async-start | bytes 2621440 | tf_op jit(solution)/shard_map/all_to_all | solution.py:172
  156.0 20.2 %all-to-all-done = bf16[16,40,1024]{2,1,0:T(8,128)(2,1)S(1)} async-done(((bf16[16,40,1024]{2,1,0:T(8,128)(2,1)}), bf16[16,40,1024]{2,1,0:T(8,128)(2,1)S(1)}, u32[]{:S(2)}, u32[]{:S(2)}) %all-to-all-start) | async-done | bytes 1310752 | tf_op jit(solution)/shard_map/all_to_all | solution.py:172
  176.1 2.8 fusion.48
  178.9 4.3 %convolution_convert_fusion = bf16[640,1024]{1,0:T(8,128)(2,1)} fusion(bf16[640,1024]{1,0:T(8,128)(2,1)S(1)} %bitcast.148, f32[640,352]{0,1:T(8,128)} %fusion.48, bf16[1,352,1024]{2,1,0:T(8,128)(2,1)S(1)} %copy-done, bf16[1,1024,352]{1,2,0:T(8,128)(2,1)} %param.37), kind=kOutput, calls=%fused_computation.27 | convolution fusion | flops 925655040 | bytes 4964352 | tf_op jit(solution)/shard_map/dot_general | solution.py:178
  183.3 8.3 %broadcast_select_fusion = bf16[2,256,64,128]{3,2,1,0:T(8,128)(2,1)} fusion(bf16[2,256,64,128]{3,2,1,0:T(8,128)(2,1)} %param.22, pred[256,64]{1,0:T(8,128)(4,1)S(1)} %copy.89, bf16[2,256,128]{2,1,0:T(8,128)(2,1)S(1)} %copy.90), kind=kLoop, calls=%fused_computation.20 | loop fusion | flops 4194304 | bytes 16924672 | tf_op jit(solution)/shard_map/jit(_where)/select_n | solution.py:142
  191.5 4.7 %gather_fusion.3 = bf16[4,2,64,128]{3,2,1,0:T(8,128)(2,1)} fusion(bf16[2,256,64,128]{3,2,1,0:T(8,128)(2,1)} %broadcast_select_fusion, s32[1024]{0:T(1024)S(1)} %pad_clamp_fusion.3), kind=kCustom, calls=%fused_computation.4 | custom fusion | bytes 262160 | tf_op jit(solution)/shard_map/gather | solution.py:208
  196.5 15.5 %scatter_custom_fusion.1 = s32[4096]{0:T(1024)S(1)} fusion(s32[4096]{0:T(1024)S(1)} %add_select_fusion.1, s32[4096]{0:T(1024)S(1)} %iota.80, s32[]{:T(128)} %constant.36.clone.1), kind=kCustom, calls=%fused_computation.136 | custom fusion | bytes 16388 | tf_op jit(solution)/shard_map/scatter | solution.py:198
  212.7 28.9 %all-reduce.5.cloned.1.call-done = bf16[16,40,1024]{2,1,0:T(8,128)(2,1)} async-done(((bf16[16,40,1024]{2,1,0:T(8,128)(2,1)}), bf16[16,40,1024]{2,1,0:T(8,128)(2,1)}) %all-reduce.5.cloned.1.call-update) | async-done | bytes 1310736 | tf_op jit(solution)/shard_map/psum | solution.py:177
  241.6 7.0 %all-to-all-start.1 = ((bf16[16,40,1024]{2,1,0:T(8,128)(2,1)}), bf16[16,40,1024]{2,1,0:T(8,128)(2,1)S(1)}, u32[]{:S(2)}, u32[]{:S(2)}) async-start(bf16[16,40,1024]{2,1,0:T(8,128)(2,1)} %all-reduce.5.cloned.1.call-done), calls=%async_computation.1 | async-start | bytes 2621440 | tf_op jit(solution)/shard_map/all_to_all | solution.py:181
  249.6 23.0 %all-to-all-done.1 = bf16[16,40,1024]{2,1,0:T(8,128)(2,1)S(1)} async-done(((bf16[16,40,1024]{2,1,0:T(8,128)(2,1)}), bf16[16,40,1024]{2,1,0:T(8,128)(2,1)S(1)}, u32[]{:S(2)}, u32[]{:S(2)}) %all-to-all-start.1) | async-done | bytes 1310752 | tf_op jit(solution)/shard_map/all_to_all | solution.py:181
  274.5 22.0 %all-gather.1 = bf16[16,4,1024]{2,1,0:T(4,128)(2,1)S(1)} all-gather(bf16[1,4,1024]{2,1,0:T(4,128)(2,1)S(1)} %bitcast.160), channel_id=2, replica_groups=mesh['req'=16,'tp'=8] {'req'}, dimensions={0}, use_global_device_ids=true | all-gather | bytes 139264 | tf_op jit(solution)/shard_map/all_gather | solution.py:210
  297.7 2.3 gather_fusion.4
  (150 shorter events, 36.9 us)
Async XLA Ops:
  8.0 170.9 %copy-start = (bf16[1,352,1024]{2,1,0:T(8,128)(2,1)S(1)}, bf16[1,352,1024]{2,1,0:T(8,128)(2,1)}, u32[]{:S(2)}) copy-start(bf16[1,352,1024]{2,1,0:T(8,128)(2,1)} %param.38) | copy-start | bytes 2162692
  8.0 130.1 %all-reduce.3.cloned.1.call-start = ((), (), s32[]{:S(2)}) async-start(), calls=%async_computation.2 | async-start | bytes 2097152 | tf_op jit(solution)/shard_map/psum | solution.py:144
  14.4 8.4 %copy-start.24 = (s32[32]{0:T(128)}, s32[32]{0:T(128)S(1)}, u32[]{:S(2)}) copy-start(s32[32]{0:T(128)S(1)} %convert_reduce_fusion) | copy-start | bytes 388
  15.9 6.9 %copy-start.29 = (s32[32]{0:T(128)}, s32[32]{0:T(128)S(1)}, u32[]{:S(2)}) copy-start(s32[32]{0:T(128)S(1)} %pad_add_fusion) | copy-start | bytes 388
  15.9 7.1 %copy-start.3 = (bf16[256,1024]{1,0:T(8,128)(2,1)S(1)}, bf16[256,1024]{1,0:T(8,128)(2,1)}, u32[]{:S(2)}) copy-start(bf16[256,1024]{1,0:T(8,128)(2,1)} %param.20) | copy-start | bytes 1572868
  15.9 7.3 %copy-start.2 = (bf16[2,8,512,128]{3,2,1,0:T(8,128)(2,1)S(1)}, bf16[2,8,512,128]{3,2,1,0:T(8,128)(2,1)}, u32[]{:S(2)}) copy-start(bf16[2,8,512,128]{3,2,1,0:T(8,128)(2,1)} %param.21) | copy-start | bytes 6291460
  23.2 16.1 %copy-start.23 = (f32[256]{0:T(256)}, f32[256]{0:T(256)S(1)}, u32[]{:S(2)}) copy-start(f32[256]{0:T(256)S(1)} %add_rsqrt_fusion.1) | copy-start | bytes 3076
  32.3 7.0 %copy-start.26 = (bf16[1024,128]{1,0:T(8,128)(2,1)S(1)}, bf16[1024,128]{1,0:T(8,128)(2,1)}, u32[]{:S(2)}) copy-start(bf16[1024,128]{1,0:T(8,128)(2,1)} %param.29) | copy-start | bytes 786436
  32.3 7.0 %copy-start.28 = (f32[1024]{0:T(1024)S(1)}, f32[1024]{0:T(1024)}, u32[]{:S(2)}) copy-start(f32[1024]{0:T(1024)} %param.28) | copy-start | bytes 12292
  32.3 7.5 %copy-start.27 = (bf16[1024,128]{1,0:T(8,128)(2,1)S(1)}, bf16[1024,128]{1,0:T(8,128)(2,1)}, u32[]{:S(2)}) copy-start(bf16[1024,128]{1,0:T(8,128)(2,1)} %param.30) | copy-start | bytes 786436
  32.3 9.2 %copy-start.21 = (f32[32,2]{0,1:T(2,128)S(1)}, f32[32,2]{0,1:T(2,128)}, u32[]{:S(2)}) copy-start(f32[32,2]{0,1:T(2,128)} %param.27) | copy-start | bytes 772
  39.3 7.3 %copy-start.8 = (s32[256,64]{0,1:T(8,128)S(1)}, s32[256,64]{0,1:T(8,128)}, u32[]{:S(2)}) copy-start(s32[256,64]{0,1:T(8,128)} %subtract_clamp_fusion.1) | copy-start | bytes 196612
  39.3 7.3 %copy-start.16 = (pred[256,64]{0,1:T(8,128)(4,1)S(1)}, pred[256,64]{0,1:T(8,128)(4,1)}, u32[]{:S(2)}) copy-start(pred[256,64]{0,1:T(8,128)(4,1)} %get-tuple-element.21) | copy-start | bytes 49156
  39.3 7.3 %copy-start.22 = (f32[32,2]{0,1:T(2,128)S(1)}, f32[32,2]{0,1:T(2,128)}, u32[]{:S(2)}) copy-start(f32[32,2]{0,1:T(2,128)} %param.27) | copy-start | bytes 772
  39.3 7.3 %copy-start.25 = (s32[32]{0:T(128)S(1)}, s32[32]{0:T(128)}, u32[]{:S(2)}) copy-start(s32[32]{0:T(128)} %copy-done.24) | copy-start | bytes 388
  39.4 7.3 %copy-start.30 = (s32[32]{0:T(128)S(1)}, s32[32]{0:T(128)}, u32[]{:S(2)}) copy-start(s32[32]{0:T(128)} %copy-done.29) | copy-start | bytes 388
  74.3 65.3 %copy-start.19 = (f32[1024]{0:T(1024)S(1)}, f32[1024]{0:T(1024)}, u32[]{:S(2)}) copy-start(f32[1024]{0:T(1024)} %param.33) | copy-start | bytes 12292
  140.4 11.6 %copy-start.9 = (s32[4096]{0:T(1024)S(1)}, s32[4096]{0:T(1024)}, u32[]{:S(2)}) copy-start(s32[4096]{0:T(1024)} %param.39) | copy-start | bytes 49156
  140.4 12.5 %copy-start.11 = (bf16[256,128]{0,1:T(8,128)(2,1)S(1)}, bf16[256,128]{0,1:T(8,128)(2,1)}, u32[]{:S(2)}) copy-start(bf16[256,128]{0,1:T(8,128)(2,1)} %convolution_convert_fusion.2) | copy-start | bytes 196612
  144.9 31.2 %all-to-all-start = ((bf16[16,40,1024]{2,1,0:T(8,128)(2,1)}), bf16[16,40,1024]{2,1,0:T(8,128)(2,1)S(1)}, u32[]{:S(2)}, u32[]{:S(2)}) async-start(bf16[16,40,1024]{2,1,0:T(8,128)(2,1)} %bitcast.149), calls=%async_computation | async-start | bytes 2621440 | tf_op jit(solution)/shard_map/all_to_all | solution.py:172
  151.9 89.7 %all-reduce.5.cloned.1.call-start = ((), (), s32[]{:S(2)}) async-start(), calls=%async_computation.3 | async-start | bytes 2621440 | tf_op jit(solution)/shard_map/psum | solution.py:177
  183.2 114.4 %all-gather.4.cloned.1.call-start = ((), (), s32[]{:S(2)}) async-start(), calls=%async_computation.4 | async-start | bytes 2228224 | tf_op jit(solution)/shard_map/all_gather | solution.py:211
  191.5 57.8 %copy-start.14 = (bf16[1024,16]{0,1:T(8,128)(2,1)S(1)}, bf16[1024,16]{0,1:T(8,128)(2,1)}, u32[]{:S(2)}) copy-start(bf16[1024,16]{0,1:T(8,128)(2,1)} %param.34) | copy-start | bytes 98308
  241.6 31.1 %all-to-all-start.1 = ((bf16[16,40,1024]{2,1,0:T(8,128)(2,1)}), bf16[16,40,1024]{2,1,0:T(8,128)(2,1)S(1)}, u32[]{:S(2)}, u32[]{:S(2)}) async-start(bf16[16,40,1024]{2,1,0:T(8,128)(2,1)} %all-reduce.5.cloned.1.call-done), calls=%async_computation.1 | async-start | bytes 2621440 | tf_op jit(solution)/shard_map/all_to_all | solution.py:181
  (12 other events, 47.2 us)
Sparse Core Ops, SparseCore 0:
  75.7 62.3 all-reduce.2
  183.3 58.1 all-reduce.4
Sparse Core Ops, SparseCore 1:
  196.3 42.1 all-gather.3
where the time goes:
time: 311 us; the launch traced here: 309 us
  waiting for transfers between devices  133 us (43%)
  local copies, waits for them, and re-layouts  59.9 us (19%)
  other arithmetic  33 us (11%)
  matrix products  31.5 us (10%)
  blocking collectives  22 us (7%)
  between operations  16.2 us (5%)
  starting transfers between devices  14.1 us (5%)
    psum x1, waiting for transfers between devices, body(): attn = lax.psum(partial_attn, 'tp')  60.5 us
    psum x1, waiting for transfers between devices, body(): lax.psum(jnp.dot(act, down_mat, preferred_element_type=jnp.float32).astyp...  28.9 us
    all_to_all x1, waiting for transfers between devices, body(): lax.all_to_all(back, 'req', split_axis=0, concat_axis=0, tiled=True)  23 us
    all_gather x1, blocking collectives, body(): lax.all_gather(send_rows, 'req', axis=0, tiled=True)  22 us
    all_to_all x1, waiting for transfers between devices, body(): lax.all_to_all(outgoing, 'req', split_axis=0, concat_axis=0, tiled=True)  20.2 us
    unnamed x68, local copies, waits for them, and re-layouts  18.9 us
    scatter x1, local copies, waits for them, and re-layouts, body(): source_of = jnp.zeros((total_reqs,), jnp.int32).at[new_slot].set(everyone)  15.5 us
    select_n x1, other arithmetic, body(): tail_new = jnp.where(write_row[None, :, :, None], fresh, tail_kv)  8.26 us
  transfers between devices with their start and end apart: 5, of which 4 were waited for; matrix products, arithmetic and copies ran while one was open for 13% of the time, Pallas kernels for 0%

commit v1 on v0

--- a/solution.py
+++ b/solution.py
@@ -141,7 +141,9 @@
     fresh = jnp.stack([key_new, value_new])[:, :, None, :]
     tail_new = jnp.where(write_row[None, :, :, None], fresh, tail_kv)
     partial_attn = jnp.dot(head_out, w_out, preferred_element_type=jnp.float32)
-    attn = lax.psum(partial_attn, "tp")
+    attn = partial_attn
+    for hop in (1, 2, 4):
+        attn = attn + lax.ppermute(attn, "tp", [(dev, dev ^ hop) for dev in range(8)])
     resid = (hidden_in.astype(jnp.float32) + attn).astype(jnp.bfloat16)
     normed2 = rms_scale(resid, ffn_gain)
     logits = jnp.dot(normed2, router_weight, preferred_element_type=jnp.float32)

time: 311 us -> 291 us (0.936)
  waiting for transfers between devices: 133 us -> 113 us
  starting transfers between devices: 14.1 us -> 17.5 us
    psum x1 -> x0, waiting for transfers between devices: 60.5 us -> none  [body(): attn = lax.psum(partial_attn, 'tp')]
    ppermute x0 -> x3, waiting for transfers between devices: none -> 49.6 us  [body(): lax.ppermute(attn, 'tp', [(dev, dev ^ hop) for dev in range(8)])]
    all_to_all x1, waiting for transfers between devices: 20.2 us -> 14.8 us  [body(): lax.all_to_all(outgoing, 'req', split_axis=0, concat_axis=0, tiled=True)]
    all_to_all x1, waiting for transfers between devices: 23 us -> 18.9 us  [body(): lax.all_to_all(back, 'req', split_axis=0, concat_axis=0, tiled=True)]
    unnamed x68 -> x48, local copies, waits for them, and re-layouts: 18.9 us -> 19.2 us
  transfers between devices with their start and end apart: 5 -> 7, of which waited for: 4 -> 6; matrix products, arithmetic and copies ran while one was open for 13% -> 14% of each run, Pallas kernels for 0% -> 0%
where the time goes in v1:
time: 291 us; the launch traced here: 289 us
  waiting for transfers between devices  113 us (39%)
  local copies, waits for them, and re-layouts  60.2 us (21%)
  other arithmetic  30.9 us (11%)
  matrix products  29.8 us (10%)
  blocking collectives  22 us (8%)
  starting transfers between devices  17.5 us (6%)
  between operations  16.1 us (6%)
    ppermute x3, waiting for transfers between devices, body(): lax.ppermute(attn, 'tp', [(dev, dev ^ hop) for dev in range(8)])  49.6 us
    psum x1, waiting for transfers between devices, body(): lax.psum(jnp.dot(act, down_mat, preferred_element_type=jnp.float32).astyp...  29.4 us
    all_gather x1, blocking collectives, body(): lax.all_gather(send_rows, 'req', axis=0, tiled=True)  22 us
    unnamed x48, local copies, waits for them, and re-layouts  19.2 us
    all_to_all x1, waiting for transfers between devices, body(): lax.all_to_all(back, 'req', split_axis=0, concat_axis=0, tiled=True)  18.9 us
    scatter x1, local copies, waits for them, and re-layouts, body(): source_of = jnp.zeros((total_reqs,), jnp.int32).at[new_slot].set(everyone)  15.5 us
    all_to_all x1, waiting for transfers between devices, body(): lax.all_to_all(outgoing, 'req', split_axis=0, concat_axis=0, tiled=True)  14.8 us
    select_n x1, other arithmetic, body(): tail_new = jnp.where(write_row[None, :, :, None], fresh, tail_kv)  8.07 us
  transfers between devices with their start and end apart: 7, of which 6 were waited for; matrix products, arithmetic and copies ran while one was open for 14% of the time, Pallas kernels for 0%

profile of v1, /device:TPU:6, one launch (start us, length us, event | category | flops | bytes accessed | tf_op | source)
XLA Modules:
  0.0 289.4 jit_solution(4810587636384097016)
XLA Ops:
  14.8 6.9 %fusion.8 = f32[2,256,512]{2,0,1:T(2,128)S(1)} fusion(s32[256,512]{1,0:T(8,128)S(1)} %subtract_clamp_fusion, s32[32]{0:T(128)S(1)} %pad_add_fusion, s32[32]{0:T(128)S(1)} %convert_reduce_fusion, f32[32,2]{0,1:T(2,128)} %param.27), kind=kOutput, calls=%fused_computation.35 | convolution fusion | flops 113246208 | bytes 1573376 | tf_op jit(solution)/shard_map/rjk,kh->hrj/dot_general | solution.py:21
  24.6 6.5 %fusion.89 = (bf16[1,256,64,128]{3,2,1,0:T(8,128)(2,1)}, bf16[1,256,64,128]{3,2,1,0:T(8,128)(2,1)}) fusion(bf16[2,256,64,128]{3,2,1,0:T(8,128)(2,1)} %param.22), kind=kLoop, calls=%fused_computation.187 | loop fusion | bytes 16777216 | tf_op jit(solution)/shard_map/slice | solution.py:59
  31.2 7.0 %copy.114 = bf16[1,256,64,128]{1,3,2,0:T(8,128)(2,1)} copy(bf16[1,256,64,128]{3,2,1,0:T(8,128)(2,1)} %get-tuple-element.12) | data formatting | bytes 8388608
  40.5 3.7 %multiply_reduce_fusion.1 = f32[2,256,64]{1,0,2:T(2,128)S(1)} fusion(bf16[2,256,64,64]{1,2,0,3:T(8,128)(2,1)} %bitcast.145, f32[2,256,64]{1,2,0:T(8,128)S(1)} %get-tuple-element.27), kind=kLoop, calls=%fused_computation.13 | loop fusion | flops 6258688 | bytes 4456448 | tf_op jit(solution)/shard_map/rhd,rthd->hrt/dot_general | solution.py:79
  47.5 2.7 fusion.4
  51.1 6.9 %copy.116 = bf16[1,256,64,128]{1,3,2,0:T(8,128)(2,1)} copy(bf16[1,256,64,128]{3,2,1,0:T(8,128)(2,1)} %get-tuple-element.13) | data formatting | bytes 8388608
  60.0 2.3 copy.115
  62.3 3.2 %multiply_reduce_fusion = f32[256,2,64]{0,2,1:T(8,128)S(1)} fusion(bf16[256,2,64,64]{0,3,1,2:T(8,128)(2,1)} %bitcast.146, f32[256,2,64]{0,1,2:T(2,128)S(1)} %bitcast_convert_fusion), kind=kLoop, calls=%fused_computation.12 | loop fusion | flops 6258688 | bytes 4456448 | tf_op jit(solution)/shard_map/hrt,rthd->rhd/dot_general | solution.py:94
  65.5 5.1 %fusion.19 = bf16[256,2,64]{0,2,1:T(8,128)(2,1)S(1)} fusion(f32[256,2,64]{0,2,1:T(8,128)S(1)} %multiply_reduce_fusion, f32[2,256,8,512]{3,1,2,0:T(8,128)} %copy-done.1, f32[2,256]{1,0:T(2,128)S(1)} %get-tuple-element.11, f32[2,256]{1,0:T(2,128)S(1)} %maximum_maximum_fusion, f32[2,256,512]{2,1,0:T(8,128)S(1)} %copy.78, ...), kind=kOutput, calls=%fused_computation.52 | convolution fusion | flops 281182208 | bytes 11802624 | tf_op jit(solution)/shard_map/hrgj,gjhd->rhd/dot_general | solution.py:93
  71.1 2.6 collective-permute-done
  74.8 24.4 %collective-permute-done.1 = f32[256,1024]{1,0:T(8,128)S(1)} collective-permute-done((f32[256,1024]{1,0:T(8,128)S(1)}, f32[256,1024]{1,0:T(8,128)S(1)}, u32[]{:S(2)}, u32[]{:S(2)}) %collective-permute-start.1) | collective-permute-done | bytes 1048608 | tf_op jit(solution)/shard_map/ppermute | solution.py:146
  102.9 22.6 %collective-permute-done.2 = f32[256,1024]{1,0:T(8,128)} collective-permute-done((f32[256,1024]{1,0:T(8,128)S(1)}, f32[256,1024]{1,0:T(8,128)}, u32[]{:S(2)}, u32[]{:S(2)}) %collective-permute-start.2) | collective-permute-done | bytes 1048608 | tf_op jit(solution)/shard_map/ppermute | solution.py:146
  129.0 3.2 %convolution_convert_fusion.1 = bf16[640,1024]{1,0:T(8,128)(2,1)} fusion(bf16[512,1024]{1,0:T(8,128)(2,1)} %reshape.353, s32[512]{0:T(512)S(1)} %multiply_add_fusion), kind=kOutput, calls=%fused_computation.28 | convolution fusion | flops 672071680 | bytes 2361344 | tf_op jit(solution)/shard_map/dot_general | solution.py:167
  132.2 8.0 %all-to-all-start = ((bf16[16,40,1024]{2,1,0:T(8,128)(2,1)}), bf16[16,40,1024]{2,1,0:T(8,128)(2,1)S(1)}, u32[]{:S(2)}, u32[]{:S(2)}) async-start(bf16[16,40,1024]{2,1,0:T(8,128)(2,1)} %bitcast.149), calls=%async_computation | async-start | bytes 2621440 | tf_op jit(solution)/shard_map/all_to_all | solution.py:174
  144.6 14.8 %all-to-all-done = bf16[16,40,1024]{2,1,0:T(8,128)(2,1)S(1)} async-done(((bf16[16,40,1024]{2,1,0:T(8,128)(2,1)}), bf16[16,40,1024]{2,1,0:T(8,128)(2,1)S(1)}, u32[]{:S(2)}, u32[]{:S(2)}) %all-to-all-start) | async-done | bytes 1310752 | tf_op jit(solution)/shard_map/all_to_all | solution.py:174
  159.4 2.8 fusion.48
  162.2 4.3 %convolution_convert_fusion = bf16[640,1024]{1,0:T(8,128)(2,1)} fusion(bf16[640,1024]{1,0:T(8,128)(2,1)S(1)} %bitcast.148, f32[640,352]{0,1:T(8,128)} %fusion.48, bf16[1,352,1024]{2,1,0:T(8,128)(2,1)S(1)} %copy-done, bf16[1,1024,352]{1,2,0:T(8,128)(2,1)} %param.37), kind=kOutput, calls=%fused_computation.27 | convolution fusion | flops 925655040 | bytes 4964352 | tf_op jit(solution)/shard_map/dot_general | solution.py:180
  166.5 8.1 %broadcast_select_fusion = bf16[2,256,64,128]{3,2,1,0:T(8,128)(2,1)} fusion(bf16[2,256,64,128]{3,2,1,0:T(8,128)(2,1)} %param.22, pred[256,64]{1,0:T(8,128)(4,1)S(1)} %copy.89, bf16[2,256,128]{2,1,0:T(8,128)(2,1)S(1)} %copy.90), kind=kLoop, calls=%fused_computation.20 | loop fusion | flops 4194304 | bytes 16924672 | tf_op jit(solution)/shard_map/jit(_where)/select_n | solution.py:142
  174.6 4.7 %gather_fusion.3 = bf16[4,2,64,128]{3,2,1,0:T(8,128)(2,1)} fusion(bf16[2,256,64,128]{3,2,1,0:T(8,128)(2,1)} %broadcast_select_fusion, s32[1024]{0:T(1024)S(1)} %pad_clamp_fusion.3), kind=kCustom, calls=%fused_computation.4 | custom fusion | bytes 262160 | tf_op jit(solution)/shard_map/gather | solution.py:210
  179.5 15.5 %scatter_custom_fusion.1 = s32[4096]{0:T(1024)S(1)} fusion(s32[4096]{0:T(1024)S(1)} %add_select_fusion.1, s32[4096]{0:T(1024)S(1)} %iota.80, s32[]{:T(128)} %constant.36.clone.1), kind=kCustom, calls=%fused_computation.136 | custom fusion | bytes 16388 | tf_op jit(solution)/shard_map/scatter | solution.py:200
  195.7 29.4 %all-reduce.2.cloned.1.call-done = bf16[16,40,1024]{2,1,0:T(8,128)(2,1)} async-done(((bf16[16,40,1024]{2,1,0:T(8,128)(2,1)}), bf16[16,40,1024]{2,1,0:T(8,128)(2,1)}) %all-reduce.2.cloned.1.call-update) | async-done | bytes 1310736 | tf_op jit(solution)/shard_map/psum | solution.py:179
  225.1 6.9 %all-to-all-start.1 = ((bf16[16,40,1024]{2,1,0:T(8,128)(2,1)}), bf16[16,40,1024]{2,1,0:T(8,128)(2,1)S(1)}, u32[]{:S(2)}, u32[]{:S(2)}) async-start(bf16[16,40,1024]{2,1,0:T(8,128)(2,1)} %all-reduce.2.cloned.1.call-done), calls=%async_computation.1 | async-start | bytes 2621440 | tf_op jit(solution)/shard_map/all_to_all | solution.py:183
  237.2 18.9 %all-to-all-done.1 = bf16[16,40,1024]{2,1,0:T(8,128)(2,1)S(1)} async-done(((bf16[16,40,1024]{2,1,0:T(8,128)(2,1)}), bf16[16,40,1024]{2,1,0:T(8,128)(2,1)S(1)}, u32[]{:S(2)}, u32[]{:S(2)}) %all-to-all-start.1) | async-done | bytes 1310752 | tf_op jit(solution)/shard_map/all_to_all | solution.py:183
  258.0 22.0 %all-gather.1 = bf16[16,4,1024]{2,1,0:T(4,128)(2,1)S(1)} all-gather(bf16[1,4,1024]{2,1,0:T(4,128)(2,1)S(1)} %bitcast.160), channel_id=2, replica_groups=mesh['req'=16,'tp'=8] {'req'}, dimensions={0}, use_global_device_ids=true | all-gather | bytes 139264 | tf_op jit(solution)/shard_map/all_gather | solution.py:212
  (135 shorter events, 40.7 us)
Async XLA Ops:
  8.0 154.2 %copy-start = (bf16[1,352,1024]{2,1,0:T(8,128)(2,1)S(1)}, bf16[1,352,1024]{2,1,0:T(8,128)(2,1)}, u32[]{:S(2)}) copy-start(bf16[1,352,1024]{2,1,0:T(8,128)(2,1)} %param.38) | copy-start | bytes 2162692
  14.7 7.1 %copy-start.3 = (bf16[256,1024]{1,0:T(8,128)(2,1)S(1)}, bf16[256,1024]{1,0:T(8,128)(2,1)}, u32[]{:S(2)}) copy-start(bf16[256,1024]{1,0:T(8,128)(2,1)} %param.20) | copy-start | bytes 1572868
  14.8 7.3 %copy-start.2 = (bf16[2,8,512,128]{3,2,1,0:T(8,128)(2,1)S(1)}, bf16[2,8,512,128]{3,2,1,0:T(8,128)(2,1)}, u32[]{:S(2)}) copy-start(bf16[2,8,512,128]{3,2,1,0:T(8,128)(2,1)} %param.21) | copy-start | bytes 6291460
  31.1 7.0 %copy-start.18 = (bf16[1024,128]{1,0:T(8,128)(2,1)S(1)}, bf16[1024,128]{1,0:T(8,128)(2,1)}, u32[]{:S(2)}) copy-start(bf16[1024,128]{1,0:T(8,128)(2,1)} %param.29) | copy-start | bytes 786436
  31.1 7.0 %copy-start.20 = (f32[1024]{0:T(1024)S(1)}, f32[1024]{0:T(1024)}, u32[]{:S(2)}) copy-start(f32[1024]{0:T(1024)} %param.28) | copy-start | bytes 12292
  31.1 7.4 %copy-start.19 = (bf16[1024,128]{1,0:T(8,128)(2,1)S(1)}, bf16[1024,128]{1,0:T(8,128)(2,1)}, u32[]{:S(2)}) copy-start(bf16[1024,128]{1,0:T(8,128)(2,1)} %param.30) | copy-start | bytes 786436
  31.1 8.6 %copy-start.17 = (f32[32,2]{0,1:T(2,128)S(1)}, f32[32,2]{0,1:T(2,128)}, u32[]{:S(2)}) copy-start(f32[32,2]{0,1:T(2,128)} %param.27) | copy-start | bytes 772
  38.1 6.1 %copy-start.10 = (s32[256,64]{0,1:T(8,128)S(1)}, s32[256,64]{0,1:T(8,128)}, u32[]{:S(2)}) copy-start(s32[256,64]{0,1:T(8,128)} %subtract_clamp_fusion.1) | copy-start | bytes 196612
  38.9 6.2 %copy-start.7 = (bf16[256,128]{0,1:T(8,128)(2,1)}, bf16[256,128]{0,1:T(8,128)(2,1)S(1)}, u32[]{:S(2)}) copy-start(bf16[256,128]{0,1:T(8,128)(2,1)S(1)} %convolution_convert_fusion.3) | copy-start | bytes 196612
  39.0 6.2 %copy-start.4 = (bf16[1,8,512,128]{2,3,1,0:T(8,128)(2,1)S(1)}, bf16[1,8,512,128]{2,3,1,0:T(8,128)(2,1)}, u32[]{:S(2)}) copy-start(bf16[1,8,512,128]{2,3,1,0:T(8,128)(2,1)} %copy.113) | copy-start | bytes 3145732
  65.5 5.2 %copy-start.9 = (bf16[128,1024]{1,0:T(8,128)(2,1)S(1)}, bf16[128,1024]{1,0:T(8,128)(2,1)}, u32[]{:S(2)}) copy-start(bf16[128,1024]{1,0:T(8,128)(2,1)} %param.32) | copy-start | bytes 786436
  70.7 30.2 %copy-start.15 = (s32[256,2]{0,1:T(2,128)S(1)}, s32[256,2]{0,1:T(2,128)}, u32[]{:S(2)}) copy-start(s32[256,2]{0,1:T(2,128)} %param.35) | copy-start | bytes 6148
  71.0 2.7 collective-permute-start
  73.9 53.0 %copy-start.16 = (f32[1024]{0:T(1024)S(1)}, f32[1024]{0:T(1024)}, u32[]{:S(2)}) copy-start(f32[1024]{0:T(1024)} %param.33) | copy-start | bytes 12292
  73.9 25.3 %collective-permute-start.1 = (f32[256,1024]{1,0:T(8,128)S(1)}, f32[256,1024]{1,0:T(8,128)S(1)}, u32[]{:S(2)}, u32[]{:S(2)}) collective-permute-start(f32[256,1024]{1,0:T(8,128)S(1)} %add.188), channel_id=1, source_target_pairs={{0,2},{1,3},{2,0},{3,1},{4,6},{5,7},{6,4},{7,5},{8,10},{9,11},{10,... | collective-permute-start | bytes 3145736 | tf_op jit(solution)/shard_map/ppermute | solution.py:146
  99.4 26.1 %collective-permute-start.2 = (f32[256,1024]{1,0:T(8,128)S(1)}, f32[256,1024]{1,0:T(8,128)}, u32[]{:S(2)}, u32[]{:S(2)}) collective-permute-start(f32[256,1024]{1,0:T(8,128)S(1)} %add.189), channel_id=1, source_target_pairs={{0,4},{1,5},{2,6},{3,7},{4,0},{5,1},{6,2},{7,3},{8,12},{9,13},{10,... | collective-permute-start | bytes 3145736 | tf_op jit(solution)/shard_map/ppermute | solution.py:146
  127.7 12.6 %copy-start.11 = (s32[4096]{0:T(1024)S(1)}, s32[4096]{0:T(1024)}, u32[]{:S(2)}) copy-start(s32[4096]{0:T(1024)} %param.39) | copy-start | bytes 49156
  127.7 13.6 %copy-start.8 = (bf16[256,128]{0,1:T(8,128)(2,1)S(1)}, bf16[256,128]{0,1:T(8,128)(2,1)}, u32[]{:S(2)}) copy-start(bf16[256,128]{0,1:T(8,128)(2,1)} %copy-done.7) | copy-start | bytes 196612
  127.7 13.6 %copy-start.13 = (bf16[256,128]{0,1:T(8,128)(2,1)S(1)}, bf16[256,128]{0,1:T(8,128)(2,1)}, u32[]{:S(2)}) copy-start(bf16[256,128]{0,1:T(8,128)(2,1)} %convolution_convert_fusion.2) | copy-start | bytes 196612
  132.2 27.1 %all-to-all-start = ((bf16[16,40,1024]{2,1,0:T(8,128)(2,1)}), bf16[16,40,1024]{2,1,0:T(8,128)(2,1)S(1)}, u32[]{:S(2)}, u32[]{:S(2)}) async-start(bf16[16,40,1024]{2,1,0:T(8,128)(2,1)} %bitcast.149), calls=%async_computation | async-start | bytes 2621440 | tf_op jit(solution)/shard_map/all_to_all | solution.py:174
  140.3 84.8 %all-reduce.2.cloned.1.call-start = ((), (), s32[]{:S(2)}) async-start(), calls=%async_computation.2 | async-start | bytes 2621440 | tf_op jit(solution)/shard_map/psum | solution.py:179
  166.5 66.6 %all-gather.4.cloned.1.call-start = ((), (), s32[]{:S(2)}) async-start(), calls=%async_computation.3 | async-start | bytes 2228224 | tf_op jit(solution)/shard_map/all_gather | solution.py:213
  174.6 58.1 %copy-start.14 = (bf16[1024,16]{0,1:T(8,128)(2,1)S(1)}, bf16[1024,16]{0,1:T(8,128)(2,1)}, u32[]{:S(2)}) copy-start(bf16[1024,16]{0,1:T(8,128)(2,1)} %param.34) | copy-start | bytes 98308
  225.1 31.0 %all-to-all-start.1 = ((bf16[16,40,1024]{2,1,0:T(8,128)(2,1)}), bf16[16,40,1024]{2,1,0:T(8,128)(2,1)S(1)}, u32[]{:S(2)}, u32[]{:S(2)}) async-start(bf16[16,40,1024]{2,1,0:T(8,128)(2,1)} %all-reduce.2.cloned.1.call-done), calls=%async_computation.1 | async-start | bytes 2621440 | tf_op jit(solution)/shard_map/all_to_all | solution.py:183
  (4 other events, 10.7 us)
Sparse Core Ops, SparseCore 0:
  166.6 58.4 all-reduce.1
Sparse Core Ops, SparseCore 1:
  179.4 42.3 all-gather.3
